TPU v7x, 32 devices: a whole 2x2x4 slice. The times are simulated.
32 devices in a mesh: slab: 8 (over z, y), rays: 4 (over x, core).
Axes of the slice: x: 2, y: 2, z: 4, core: 2. Of those that a mesh axis runs over, the one named last changes fastest.
Arguments:
- geometry: float32 [6, 4, 128], P(None, 'rays'), may hold values from -1 to 1
- entry: int32 [8, 4, 128], P('slab', 'rays'), may hold values from 0 to 63
- counts: int32 [8, 4, 128], P('slab', 'rays'), may hold values from 0 to 8
- targets: float32 [3, 4, 128], P(None, 'rays', 'slab'), may hold values from 0 to 1
- w_in: float32 [8, 256, 256], P('slab'), may hold values from -0.375 to 0.375
- w_mid: float32 [8, 2, 256, 256], P('slab'), may hold values from -0.375 to 0.375
- w_out: float32 [8, 4, 256], P('slab'), may hold values from -0.375 to 0.375
- b_hid: float32 [8, 3, 256], P('slab'), may hold values from -3 to 3
- b_out: float32 [8, 4], P('slab'), may hold values from -3 to 3
- freqs: float32 [8, 3, 128], P('slab'), may hold values from -3 to 3
Outputs:
- pixels: float32 [3, 4, 128], P(None, 'rays', 'slab')
- grad_in: float32 [8, 256, 256], P('slab')
- grad_mid: float32 [8, 2, 256, 256], P('slab')
- grad_out: float32 [8, 4, 256], P('slab')
- grad_hid: float32 [8, 3, 256], P('slab')
- grad_bout: float32 [8, 4], P('slab')
Inputs may be any that keep to these rules, and one draw needn't show every extreme that they name: `entry`: the index of a ray's first sample in a slab. `counts`: how many of the 8 slots of a ray lie inside a slab; 0 where the ray misses it.
All inputs are finite; a program needn't handle non-finite values.
Results may differ from a plain program's by a relative error of at most 0.0003.
Values sent between devices are 32-bit elements; how exact they have to be, the bound alone decides.
A program may use at most 128 MiB of HBM per device.

v0:
```python
import math

import jax
import jax.numpy as jnp
from jax import lax
from jax.sharding import PartitionSpec as P

MID = 2
SAMP = 8
RAY_DEV = 16


HIGH = lax.Precision.HIGHEST


def features(freqs, geometry, entry):
    width = geometry.shape[1]
    slots = jnp.arange(SAMP, dtype=jnp.int32)[:, None]
    times = 0.25 * (entry.astype(jnp.float32)[None, :] + slots.astype(jnp.float32) + 0.5)
    places = geometry[0:3, None, :] + times[None] * geometry[3:6, None, :]
    places = places.reshape(3, SAMP * width)
    phase = jnp.einsum("dk,dn->nk", freqs, places, precision=HIGH)
    return jnp.concatenate([jnp.sin(phase), jnp.cos(phase)], axis=1)


def hidden_layer(hidden, weight, bias):
    return jax.nn.softplus(jnp.dot(hidden, weight, precision=HIGH) + bias)


def head(hidden, w_out, b_out, counts, delta):
    width = counts.shape[0]
    slots = jnp.arange(SAMP, dtype=jnp.int32)[:, None]
    result = jnp.einsum("ch,nh->cn", w_out, hidden, precision=HIGH) + b_out[:, None]
    sigma = jax.nn.softplus(result[0]).reshape(SAMP, width)
    colors = jax.nn.sigmoid(result[1:]).reshape(3, SAMP, width)
    alive = slots < counts[None, :]
    depth = jnp.where(alive, sigma * delta, jnp.float32(0.0))
    before = jnp.cumsum(depth, axis=0) - depth
    weights = jnp.exp(-before) * (1.0 - jnp.exp(-depth))
    color = jnp.sum(weights[None] * colors, axis=1)
    logtrans = -jnp.sum(depth, axis=0)
    return jnp.concatenate([color, logtrans[None]], axis=0)


def segment(params, encoded, counts, delta):
    hidden = hidden_layer(encoded, params[0], params[3][0])
    for layer in range(MID):
        hidden = hidden_layer(hidden, params[1][layer], params[3][layer + 1])
    return head(hidden, params[2], params[4], counts, delta)


def composite(segments, targets, factor):
    logtrans = segments[3]
    before = jnp.cumsum(logtrans, axis=0) - logtrans
    shade = jnp.exp(before)
    pixels = jnp.sum(shade[None] * segments[:3], axis=1) + jnp.exp(jnp.sum(logtrans, axis=0))[None]
    loss = factor * jnp.sum((pixels - targets) ** 2)
    return (loss, pixels)


def shards(geometry, entry, counts, targets, w_in, w_mid, w_out, b_hid, b_out, freqs):
    slabs = lax.axis_size("slab")
    delta = 3.0 / (SAMP * slabs)
    factor = 1.0 / math.sqrt(3.0 * lax.axis_size("rays") * slabs * RAY_DEV)
    local_geometry = geometry[:, 0, :]
    local_entry = entry[0, 0]
    local_counts = counts[0, 0]
    local_targets = targets[:, 0, :]
    params = (w_in[0], w_mid[0], w_out[0], b_hid[0], b_out[0])
    encoded = features(freqs[0], local_geometry, local_entry)
    seg, pull_all = jax.vjp(lambda p: segment(p, encoded, local_counts, delta), params)
    owned = lax.all_to_all(seg[:, None, :], "slab", split_axis=2, concat_axis=1, tiled=True)
    loss, pullback, pixels = jax.vjp(
        lambda s: composite(s, local_targets, factor), owned, has_aux=True
    )
    owned_adjoint = pullback(jnp.ones((), jnp.float32))[0]
    adjoint = lax.all_to_all(owned_adjoint, "slab", split_axis=1, concat_axis=2, tiled=True)[
        :, 0, :
    ]
    grads = pull_all(adjoint)[0]
    grad_in, grad_mid, grad_out, grad_hid, grad_bout = lax.psum(
        (grads[0], grads[1], grads[2], grads[3], grads[4]), "rays"
    )
    return (
        pixels[:, None, :],
        grad_in[None],
        grad_mid[None],
        grad_out[None],
        grad_hid[None],
        grad_bout[None],
    )


def solution(mesh):
    in_specs = (
        P(None, "rays", None),
        P("slab", "rays", None),
        P("slab", "rays", None),
        P(None, "rays", "slab"),
        P("slab", None, None),
        P("slab", None, None, None),
        P("slab", None, None),
        P("slab", None, None),
        P("slab", None),
        P("slab", None, None),
    )
    out_specs = (
        P(None, "rays", "slab"),
        P("slab", None, None),
        P("slab", None, None, None),
        P("slab", None, None),
        P("slab", None, None),
        P("slab", None),
    )
    return jax.shard_map(shards, mesh=mesh, in_specs=in_specs, out_specs=out_specs, check_vma=False)
```

profile of v0, /device:TPU:0, one launch (start us, length us, event | category | flops | bytes accessed | tf_op | source)
XLA Modules:
  0.0 106.8 jit_solution(6340818017745772977)
XLA Ops:
  7.2 0.7 copy-done.9
  7.9 0.7 copy-done.3
  8.7 0.7 copy-done.4
  9.4 5.2 %fusion.69 = (f32[1024,128]{0,1:T(8,128)S(1)}, f32[1024,128]{0,1:T(8,128)S(1)}) fusion(f32[1,3,128]{2,0,1:T(1,128)S(1)} %copy-done.4, f32[1,3,8,128]{3,2,1,0:T(8,128)S(1)} %add_bitcast_fusion.1), kind=kOutput, calls=%fused_computation.129 | convolution fusion | flops 4718592 | bytes 1062400 | tf_op jit(solution)/shard_map/dk,dn->nk/dot_general | solution.py:22
  14.6 1.8 %convolution_add_fusion.2 = f32[1024,256]{1,0:T(8,128)S(1)} fusion(f32[1024,128]{0,1:T(8,128)S(1)} %get-tuple-element.64, f32[1024,128]{0,1:T(8,128)S(1)} %get-tuple-element.63, f32[256]{0:T(256)S(1)} %bitcast.147, f32[1,256,256]{2,1,0:T(8,128)S(1)} %copy-done), kind=kOutput, calls=%fused_computation.14 | convolution fusion | flops 805830656 | bytes 2360320 | tf_op jit(solution)/shard_map/jvp()/dot_general | solution.py:27
  16.4 1.4 %convolution_add_fusion.1 = f32[1024,256]{1,0:T(8,128)S(1)} fusion(f32[1024,256]{1,0:T(8,128)S(1)} %convolution_add_fusion.2, f32[256]{0:T(256)S(1)} %bitcast.156, f32[1,2,256,256]{3,2,1,0:T(8,128)S(1)} %copy-done.7), kind=kOutput, calls=%fused_computation.13 | convolution fusion | flops 807141376 | bytes 2360320 | tf_op jit(solution)/shard_map/jvp()/dot_general | solution.py:27
  17.9 1.5 %convolution_add_fusion = f32[1024,256]{1,0:T(8,128)S(1)} fusion(f32[1024,256]{1,0:T(8,128)S(1)} %convolution_add_fusion.1, f32[256]{0:T(256)S(1)} %bitcast.155, f32[1,2,256,256]{3,2,1,0:T(8,128)S(1)} %copy-done.7), kind=kOutput, calls=%fused_computation.12 | convolution fusion | flops 807141376 | bytes 2360320 | tf_op jit(solution)/shard_map/jvp()/dot_general | solution.py:27
  19.4 0.7 copy-done.10
  20.0 1.5 %fusion = f32[4,1024]{1,0:T(4,128)S(1)} fusion(f32[1024,256]{1,0:T(8,128)S(1)} %convolution_add_fusion, f32[4]{0:T(128)S(1)} %bitcast.157, f32[1,4,256]{2,1,0:T(4,128)S(1)} %copy-done.8), kind=kOutput, calls=%fused_computation.19 | convolution fusion | flops 14159872 | bytes 1069072 | tf_op jit(solution)/shard_map/jvp(ch,nh->cn)/dot_general | solution.py:33
  21.6 0.6 copy-done.5
  22.4 0.8 copy.29
  23.1 7.3 %all-to-all-start = ((f32[4,1,128]{0,1,2:T(1,128)}), f32[4,1,128]{0,1,2:T(1,128)S(1)}, u32[]{:S(2)}, u32[]{:S(2)}) async-start(f32[4,1,128]{0,1,2:T(1,128)} %bitcast.13), calls=%async_computation | async-start | bytes 131072 | tf_op jit(solution)/shard_map/all_to_all | solution.py:72
  30.5 6.9 %all-to-all-done = f32[4,1,128]{0,1,2:T(1,128)S(1)} async-done(((f32[4,1,128]{0,1,2:T(1,128)}), f32[4,1,128]{0,1,2:T(1,128)S(1)}, u32[]{:S(2)}, u32[]{:S(2)}) %all-to-all-start) | async-done | bytes 2080 | tf_op jit(solution)/shard_map/all_to_all | solution.py:72
  37.3 1.8 %slice_reduce_fusion = f32[128]{0:T(128)S(1)} fusion(f32[4,1,128]{0,1,2:T(1,128)S(1)} %all-to-all-done), kind=kLoop, calls=%fused_computation.44 | loop fusion | bytes 1024 | tf_op jit(solution)/shard_map/jvp()/slice | solution.py:53
  39.6 0.7 copy-done.6
  40.6 0.6 copy.31
  41.2 3.3 %all-to-all-start.1 = ((f32[4,8,16]{2,0,1:T(4,128)}), f32[4,8,16]{2,0,1:T(4,128)S(1)}, u32[]{:S(2)}, u32[]{:S(2)}) async-start(f32[4,8,16]{2,0,1:T(4,128)} %copy.31), calls=%async_computation.1 | async-start | bytes 32768 | tf_op jit(solution)/shard_map/all_to_all | solution.py:77
  44.5 0.2 all-reduce.13.cloned.1.call-start
  44.8 6.3 %all-to-all-done.1 = f32[4,8,16]{2,0,1:T(4,128)S(1)} async-done(((f32[4,8,16]{2,0,1:T(4,128)}), f32[4,8,16]{2,0,1:T(4,128)S(1)}, u32[]{:S(2)}, u32[]{:S(2)}) %all-to-all-start.1) | async-done | bytes 2080 | tf_op jit(solution)/shard_map/all_to_all | solution.py:77
  51.4 3.0 %fusion.75 = (f32[256]{0:T(256)S(1)}, f32[1024,256]{1,0:T(8,128)S(1)}) fusion(f32[1024,256]{1,0:T(8,128)} %copy-done.13, f32[1,4,256]{2,1,0:T(4,128)S(1)} %copy-done.8, f32[1,1024]{1,0:T(1,128)S(1)} %fusion.36, f32[3,1024]{1,0:T(4,128)S(1)} %get-tuple-element.65), kind=kOutput, calls=%fused_computation.135 | convolution fusion | flops 15994624 | bytes 2118656 | tf_op jit(solution)/shard_map/transpose(jvp(ch,nh->cn))/dot_general | solution.py:33
  54.5 2.3 %convolution_bitcast_fusion.1 = f32[1,256,256]{2,1,0:T(8,128)S(1)} fusion(f32[1024,256]{1,0:T(8,128)S(1)} %get-tuple-element.80, f32[1024,256]{1,0:T(8,128)S(1)} %copy-done.12), kind=kOutput, calls=%fused_computation.16 | convolution fusion | flops 806879232 | bytes 2359296 | tf_op jit(solution)/shard_map/transpose(jvp())/dot_general | solution.py:27
  56.7 1.7 %fusion.74 = (f32[256]{0:T(256)S(1)}, f32[1024,256]{1,0:T(8,128)S(1)}) fusion(f32[1024,256]{1,0:T(8,128)S(1)} %copy-done.12, f32[1024,256]{1,0:T(8,128)S(1)} %get-tuple-element.80, f32[1,2,256,256]{3,2,1,0:T(8,128)S(1)} %copy-done.7), kind=kOutput, calls=%fused_computation.134 | convolution fusion | flops 808713984 | bytes 3408896 | tf_op jit(solution)/shard_map/transpose(jvp())/dot_general | solution.py:27
  58.4 2.3 %convolution_bitcast_fusion = f32[1,256,256]{2,1,0:T(8,128)S(1)} fusion(f32[1024,256]{1,0:T(8,128)S(1)} %get-tuple-element.78, f32[1024,256]{1,0:T(8,128)S(1)} %convolution_add_fusion.2), kind=kOutput, calls=%fused_computation.15 | convolution fusion | flops 806879232 | bytes 2359296 | tf_op jit(solution)/shard_map/transpose(jvp())/dot_general | solution.py:27
  60.7 1.7 %fusion.73 = (f32[256]{0:T(256)S(1)}, f32[1024,256]{1,0:T(8,128)S(1)}) fusion(f32[1024,256]{1,0:T(8,128)S(1)} %convolution_add_fusion.2, f32[1024,256]{1,0:T(8,128)S(1)} %get-tuple-element.78, f32[1,2,256,256]{3,2,1,0:T(8,128)S(1)} %copy-done.7), kind=kOutput, calls=%fused_computation.133 | convolution fusion | flops 808713984 | bytes 3408896 | tf_op jit(solution)/shard_map/transpose(jvp())/dot_general | solution.py:27
  62.4 1.7 %convolution_bitcast_fusion.2 = f32[1,256,256]{2,1,0:T(8,128)} fusion(f32[1024,256]{1,0:T(8,128)S(1)} %get-tuple-element.76, f32[1024,128]{0,1:T(8,128)S(1)} %get-tuple-element.64, f32[1024,128]{0,1:T(8,128)S(1)} %get-tuple-element.63), kind=kOutput, calls=%fused_computation.17 | convolution fusion | flops 805568512 | bytes 2359296 | tf_op jit(solution)/shard_map/transpose(jvp())/dot_general | solution.py:27
  64.1 0.8 add_bitcast_fusion
  65.0 0.6 copy.33
  65.7 1.1 convolution_bitcast_fusion.3
  66.7 6.9 %all-reduce.9 = (f32[1,4,256]{2,1,0:T(4,128)}, f32[1,3,256]{2,0,1:T(1,128)}, f32[1,4]{1,0:T(1,128)}) all-reduce(f32[1,4,256]{2,1,0:T(4,128)S(1)} %convolution_bitcast_fusion.3, f32[1,3,256]{2,0,1:T(1,128)S(1)} %broadcast_in_dim.83, f32[1,4]{1,0:T(1,128)S(1)} %bitcast.151), channel_id=1, replica_groups=mesh['slab'=8,'rays'=4] {'rays'}, use_global_device_ids=true, to_apply=%region_13.15 | all-reduce | flops 1796 | bytes 14368 | tf_op jit(solution)/shard_map/psum | solution.py:81
  73.7 23.7 %all-reduce.13.cloned.1.call-done = (f32[1,256,256]{2,1,0:T(8,128)}, f32[1,2,256,256]{3,2,1,0:T(8,128)}) async-done(((f32[1,256,256]{2,1,0:T(8,128)}, f32[1,2,256,256]{3,2,1,0:T(8,128)}), (f32[1,256,256]{2,1,0:T(8,128)}, f32[1,2,256,256]{3,2,1,0:T(8,128)})) %all-reduce.13.cloned.1.call-update) | async-done | bytes 786448 | tf_op jit(solution)/shard_map/psum | solution.py:81
  97.4 1.7 %copy.76 = f32[1,256,256]{2,1,0:T(8,128)} copy(f32[1,256,256]{2,1,0:T(8,128)} %get-tuple-element.84) | data formatting | bytes 524288
  99.1 0.8 copy.77
  (75 shorter events, 1.5 us)
Async XLA Ops:
  7.2 7.4 %copy-start = (f32[1,256,256]{2,1,0:T(8,128)S(1)}, f32[1,256,256]{2,1,0:T(8,128)}, u32[]{:S(2)}) copy-start(f32[1,256,256]{2,1,0:T(8,128)} %param.15) | copy-start | bytes 786436
  7.2 0.7 copy-start.9
  7.2 0.7 copy-start.2
  7.9 0.7 copy-start.3
  8.7 0.7 copy-start.4
  14.5 1.8 %copy-start.7 = (f32[1,2,256,256]{3,2,1,0:T(8,128)S(1)}, f32[1,2,256,256]{3,2,1,0:T(8,128)}, u32[]{:S(2)}) copy-start(f32[1,2,256,256]{3,2,1,0:T(8,128)} %param.16) | copy-start | bytes 1572868
  17.8 1.5 %copy-start.11 = (f32[1024,256]{1,0:T(8,128)}, f32[1024,256]{1,0:T(8,128)S(1)}, u32[]{:S(2)}) copy-start(f32[1024,256]{1,0:T(8,128)S(1)} %convolution_add_fusion.1) | copy-start | bytes 3145732
  17.9 1.5 %copy-start.8 = (f32[1,4,256]{2,1,0:T(4,128)S(1)}, f32[1,4,256]{2,1,0:T(4,128)}, u32[]{:S(2)}) copy-start(f32[1,4,256]{2,1,0:T(4,128)} %param.17) | copy-start | bytes 12292
  19.3 2.2 %copy-start.13 = (f32[1024,256]{1,0:T(8,128)}, f32[1024,256]{1,0:T(8,128)S(1)}, u32[]{:S(2)}) copy-start(f32[1024,256]{1,0:T(8,128)S(1)} %convolution_add_fusion) | copy-start | bytes 3145732
  19.3 0.7 copy-start.10
  21.6 0.7 copy-start.5
  23.1 14.2 %all-to-all-start = ((f32[4,1,128]{0,1,2:T(1,128)}), f32[4,1,128]{0,1,2:T(1,128)S(1)}, u32[]{:S(2)}, u32[]{:S(2)}) async-start(f32[4,1,128]{0,1,2:T(1,128)} %bitcast.13), calls=%async_computation | async-start | bytes 131072 | tf_op jit(solution)/shard_map/all_to_all | solution.py:72
  39.6 0.7 copy-start.6
  41.2 9.9 %all-to-all-start.1 = ((f32[4,8,16]{2,0,1:T(4,128)}), f32[4,8,16]{2,0,1:T(4,128)S(1)}, u32[]{:S(2)}, u32[]{:S(2)}) async-start(f32[4,8,16]{2,0,1:T(4,128)} %copy.31), calls=%async_computation.1 | async-start | bytes 32768 | tf_op jit(solution)/shard_map/all_to_all | solution.py:77
  44.5 52.9 %all-reduce.13.cloned.1.call-start = ((), (), s32[]{:S(2)}) async-start(), calls=%async_computation.2 | async-start | bytes 1572864 | tf_op jit(solution)/shard_map/psum | solution.py:81
  51.4 3.0 %copy-start.12 = (f32[1024,256]{1,0:T(8,128)S(1)}, f32[1024,256]{1,0:T(8,128)}, u32[]{:S(2)}) copy-start(f32[1024,256]{1,0:T(8,128)} %copy-done.11) | copy-start | bytes 3145732
  64.1 1.6 %copy-start.14 = (f32[1024,256]{1,0:T(8,128)S(1)}, f32[1024,256]{1,0:T(8,128)}, u32[]{:S(2)}) copy-start(f32[1024,256]{1,0:T(8,128)} %copy-done.13) | copy-start | bytes 3145732
  97.4 1.7 %copy-start.1 = (f32[1,2,256,256]{3,2,1,0:T(8,128)S(1)}, f32[1,2,256,256]{3,2,1,0:T(8,128)}, u32[]{:S(2)}) copy-start(f32[1,2,256,256]{3,2,1,0:T(8,128)} %get-tuple-element.85) | copy-start | bytes 1572868
Sparse Core Ops, SparseCore 0:
  65.1 32.2 all-reduce.12
where the time goes:
time: 107 us
  waiting for transfers between devices  36.9 us (34%)
  matrix products  25.1 us (23%)
  between operations  14.4 us (13%)
  local copies, waits for them, and re-layouts  11.1 us (10%)
  starting transfers between devices  10.9 us (10%)
  blocking collectives  6.95 us (6%)
  other arithmetic  1.54 us (1%)
    psum x1, waiting for transfers between devices, shards(): lax.psum((grads[0], grads[1], grads[2], grads[3], grads[4]), 'rays')  23.7 us
    dot_general x8, matrix products, hidden_layer(): return jax.nn.softplus(jnp.dot(hidden, weight, precision=HIGH) + bias)  14.3 us
    all_to_all x1, starting transfers between devices, shards(): lax.all_to_all(seg[:, None, :], 'slab', split_axis=2, concat_axis=1, tile...  7.31 us
    unnamed x36, local copies, waits for them, and re-layouts  7.28 us
    psum x1, blocking collectives, shards(): lax.psum((grads[0], grads[1], grads[2], grads[3], grads[4]), 'rays')  6.95 us
    all_to_all x1, waiting for transfers between devices, shards(): lax.all_to_all(seg[:, None, :], 'slab', split_axis=2, concat_axis=1, tile...  6.88 us
    all_to_all x1, waiting for transfers between devices, shards(): lax.all_to_all(owned_adjoint, 'slab', split_axis=1, concat_axis=2, tiled=...  6.27 us
    dot_general x3, matrix products, head(): jnp.einsum('ch,nh->cn', w_out, hidden, precision=HIGH) + b_out[:, None]  5.6 us
  transfers between devices with their start and end apart: 3, of which 3 were waited for; matrix products, arithmetic and copies ran while one was open for 2% of the time, Pallas kernels for 0%

commit v1 on v0

v1 whole, which is shorter than its diff:
```python
import functools
import math

import jax
import jax.numpy as jnp
from jax import lax
from jax.experimental import pallas as pl
from jax.experimental.pallas import tpu as pltpu
from jax.sharding import PartitionSpec as P

SAMP = 8
F32 = jnp.float32
BF16 = jnp.bfloat16
MESH = pl.DeviceIdType.MESH
NT = (((1,), (1,)), ((), ()))


def split(x):
    hi = x.astype(BF16)
    return hi, (x - hi.astype(F32)).astype(BF16)


def mm(a, b):
    return jnp.dot(a, b, preferred_element_type=F32)


def mm_nt(a, b):
    return lax.dot_general(a, b, NT, preferred_element_type=F32)


def softplus(z):
    return jnp.maximum(z, 0.0) + jnp.log1p(jnp.exp(-jnp.abs(z)))


def sincos(x):
    k = jnp.round(x * F32(2.0 / math.pi))
    r = ((x - k * F32(1.5703125)) - k * F32(4.837512969970703e-4)) - k * F32(7.549789954891882e-8)
    q = k.astype(jnp.int32)
    r2 = r * r
    s = r + r * r2 * (F32(-1.6666654611e-1) + r2 * (F32(8.3321608736e-3) + r2 * F32(-1.9515295891e-4)))
    c = F32(1.0) - F32(0.5) * r2 + r2 * r2 * (
        F32(4.166664568298827e-2) + r2 * (F32(-1.388731625493765e-3) + r2 * F32(2.443315711809948e-5))
    )
    odd = (q & 1) == 1
    sn = jnp.where(odd, c, s)
    cs = jnp.where(odd, s, c)
    sn = jnp.where((q & 2) == 2, -sn, sn)
    cs = jnp.where(((q + 1) & 2) == 2, -cs, cs)
    return sn, cs


def kernel(
    slabs, n_rays, delta, factor,
    geo_ref, ent_ref, cnt_ref, tgt_ref, win_ref, wmid_ref, wout_ref, bhid_ref, bout_ref, fr_ref,
    pix_ref, gin_ref, gmid_ref, gout_ref, ghid_ref, gbout_ref,
    hh, hl, sg, dh, dl, wt, wn, seg_all, g, recv_a, recv_b, part, fin,
    seg_send, seg_recv, a_send, a_recv, b_send, b_recv, c_send, c_recv,
):
    me = lax.axis_index("slab")
    ray = lax.axis_index("rays")
    core = lax.rem(ray, 2)
    width = geo_ref.shape[2]
    own = tgt_ref.shape[2]
    n = SAMP * width
    hid = win_ref.shape[2]
    fe = fr_ref.shape[2]
    mid = wmid_ref.shape[1]
    layers = mid + 1
    bits = [b for b in range(1, 16) if (1 << b) < n_rays]
    chunk = 256
    n_chunks = n // chunk

    barrier = pltpu.get_barrier_semaphore()
    for k in range(1, slabs):
        pl.semaphore_signal(barrier, inc=1, device_id=(lax.rem(me + k, slabs), ray), device_id_type=MESH)
    peers = [1] + [1 << b for b in bits]

    def other(bit):
        place = lax.rem(ray // bit, 2)
        return ray + bit * (1 - 2 * place)

    for bit in peers:
        pl.semaphore_signal(barrier, inc=1, device_id=(me, other(bit)), device_id_type=MESH)

    def chunks(body):
        if n_chunks <= 4:
            for i in range(n_chunks):
                body(i * chunk)
        else:
            def step(i, carry):
                body(pl.multiple_of(i * chunk, chunk))
                return carry
            lax.fori_loop(0, n_chunks, step, 0)

    for l in range(layers):
        w = win_ref[0] if l == 0 else wmid_ref[0, l - 1]
        hi, lo = split(w.T)
        wt[l, 0] = hi
        wt[l, 1] = lo
        if l > 0:
            hi, lo = split(w)
            wn[l - 1, 0] = hi
            wn[l - 1, 1] = lo

    pad5 = jnp.zeros((8 - layers, hid), F32)
    bias = jnp.concatenate([bhid_ref[0], pad5], axis=0).T
    freq = jnp.concatenate([fr_ref[0], jnp.zeros((5, fe), F32)], axis=0).T

    geo = geo_ref[:, 0, :]
    t0 = 0.25 * (ent_ref[0].astype(F32) + 0.5)
    base = jnp.zeros((fe, width), F32)
    turn = jnp.zeros((fe, width), F32)
    for d in range(3):
        dirs = geo[3 + d:4 + d, :]
        place = geo[d:d + 1, :] + t0 * dirs
        base = base + freq[:, d:d + 1] * place
        turn = turn + freq[:, d:d + 1] * (0.25 * dirs)
    sn, cs = sincos(base)
    sd, cd = sincos(turn)
    for j in range(SAMP):
        lanes = slice(j * width, (j + 1) * width)
        hi, lo = split(sn)
        hh[0, 0:fe, lanes] = hi
        hl[0, 0:fe, lanes] = lo
        hi, lo = split(cs)
        hh[0, fe:2 * fe, lanes] = hi
        hl[0, fe:2 * fe, lanes] = lo
        if j < SAMP - 1:
            sn, cs = sn * cd + cs * sd, cs * cd - sn * sd

    for l in range(layers):
        def layer(at, l=l):
            lanes = pl.ds(at, chunk)
            hi = hh[l, :, lanes]
            z = mm(wt[l, 0], hi) + mm(wt[l, 1], hi) + mm(wt[l, 0], hl[l, :, lanes])
            z = z + bias[:, l:l + 1]
            h = softplus(z)
            sg[l, :, lanes] = jnp.exp(z - h)
            hi, lo = split(h)
            hh[l + 1, :, lanes] = hi
            hl[l + 1, :, lanes] = lo
        chunks(layer)

    wo = jnp.concatenate([wout_ref[0], jnp.zeros((4, hid), F32)], axis=0)
    wo_hi, wo_lo = split(wo)
    last_hi = hh[layers]
    out = mm(wo_hi, last_hi) + mm(wo_lo, last_hi) + mm(wo_hi, hl[layers])
    bout = jnp.concatenate([bout_ref[...], jnp.zeros((7, 4), F32)], axis=0)
    counts = cnt_ref[0]
    sigma = softplus(out[0:1] + bout[0:1, 0:1])
    sigma_slope = jnp.exp(out[0:1] + bout[0:1, 0:1] - sigma)
    rgb = []
    for c in range(3):
        o = out[c + 1:c + 2] + bout[0:1, c + 1:c + 2]
        rgb.append(jnp.exp(o - softplus(o)))
    rgb = jnp.concatenate(rgb, axis=0)
    before = jnp.zeros((1, width), F32)
    color = jnp.zeros((3, width), F32)
    weight, after, live, tints = [], [], [], []
    for j in range(SAMP):
        lanes = slice(j * width, (j + 1) * width)
        alive = counts > j
        tau = jnp.where(alive, sigma[:, lanes] * delta, 0.0)
        e0 = jnp.exp(-before)
        e1 = jnp.exp(-tau)
        w = e0 * (1.0 - e1)
        tint = rgb[:, lanes]
        color = color + w * tint
        before = before + tau
        weight.append(w)
        after.append(e0 * e1)
        live.append(alive)
        tints.append(tint)
    mine = lax.broadcasted_iota(jnp.int32, (own, width), 1) == (
        lax.broadcasted_iota(jnp.int32, (own, width), 0) + me * own
    )
    spread = jnp.where(mine, 1.0, 0.0).astype(F32)
    spot = jnp.dot(tgt_ref[:, 0, :], spread, precision=lax.Precision.HIGHEST, preferred_element_type=F32)
    seg_all[me] = jnp.concatenate([color, -before, spot, jnp.zeros((1, width), F32)], axis=0)

    pl.semaphore_wait(barrier, slabs - 1 + len(peers))
    copies = []
    for k in range(1, slabs):
        copy = pltpu.make_async_remote_copy(
            src_ref=seg_all.at[me], dst_ref=seg_all.at[me],
            send_sem=seg_send.at[k], recv_sem=seg_recv.at[k],
            device_id=(lax.rem(me + k, slabs), ray), device_id_type=MESH,
        )
        copy.start()
        copies.append(copy)
    for copy in copies:
        copy.wait()

    total = jnp.zeros((1, width), F32)
    pixels = jnp.zeros((3, width), F32)
    target = jnp.zeros((3, width), F32)
    shades, colors = [], []
    mine_shade = jnp.zeros((1, width), F32)
    for s in range(slabs):
        block = seg_all[s]
        shade = jnp.exp(total)
        pixels = pixels + shade * block[0:3]
        target = target + block[4:7]
        total = total + block[3:4]
        mine_shade = mine_shade + jnp.where(me == s, shade, 0.0)
        shades.append(shade)
        colors.append(block[0:3])
    clear = jnp.exp(total)
    pixels = pixels + clear
    pull = (2.0 * factor) * (pixels - target)
    d_log = clear * jnp.sum(pull, axis=0, keepdims=True)
    for s in range(slabs):
        term = shades[s] * jnp.sum(pull * colors[s], axis=0, keepdims=True)
        d_log = d_log + jnp.where(me < s, term, 0.0)
    d_color = mine_shade * pull
    pix_ref[:, 0, :] = lax.dot_general(
        pixels, spread, NT, precision=lax.Precision.HIGHEST, preferred_element_type=F32
    )

    later = jnp.zeros((1, width), F32)
    d_out = [None] * SAMP
    for j in reversed(range(SAMP)):
        lanes = slice(j * width, (j + 1) * width)
        u = jnp.sum(d_color * tints[j], axis=0, keepdims=True)
        d_tau = after[j] * u - later - d_log
        later = later + weight[j] * u
        d0 = jnp.where(live[j], d_tau * delta * sigma_slope[:, lanes], 0.0)
        d_rgb = d_color * weight[j] * tints[j] * (1.0 - tints[j])
        d_out[j] = jnp.concatenate([d0, d_rgb, jnp.zeros((4, width), F32)], axis=0)
    d_out = jnp.concatenate(d_out, axis=1)
    do_hi, do_lo = split(d_out)
    wot_hi, wot_lo = split(wo.T)

    def last(at):
        lanes = pl.ds(at, chunk)
        hi, lo = (d_hi_ref(at), d_lo_ref(at))
        d = mm(wot_hi, hi) + mm(wot_lo, hi) + mm(wot_hi, lo)
        hi, lo = split(d * sg[layers - 1, :, lanes])
        dh[0, :, lanes] = hi
        dl[0, :, lanes] = lo

    dh[1, 0:8, :] = do_hi
    dl[1, 0:8, :] = do_lo

    def d_hi_ref(at):
        return dh[1, 0:8, pl.ds(at, chunk)]

    def d_lo_ref(at):
        return dl[1, 0:8, pl.ds(at, chunk)]

    small = hid
    ones = jnp.ones((16, n), BF16)
    g[layers - 1, small:small + 16, :] = jnp.zeros((16, hid), F32)
    g_out = mm_nt(do_hi, last_hi) + mm_nt(do_lo, last_hi) + mm_nt(do_hi, hl[layers])
    g[layers - 1, small:small + 4, :] = g_out[0:4]
    row = mm_nt(ones, do_hi) + mm_nt(ones, do_lo)
    g[layers - 1, small + 7:small + 8, 0:8] = row[0:1, 0:8]
    chunks(last)

    def rows_of(b):
        return hid + 16 if b == layers - 1 else hid

    def stage_a(b):
        half = rows_of(b) // 2
        return pltpu.make_async_remote_copy(
            src_ref=g.at[b, pl.ds(pl.multiple_of((1 - core) * half, 8), half)],
            dst_ref=recv_a.at[b, pl.ds(0, half)],
            send_sem=a_send.at[b], recv_sem=a_recv.at[b],
            device_id=(me, other(1)), device_id_type=MESH,
        )

    def stage_b(b, i):
        half = rows_of(b) // 2
        return pltpu.make_async_remote_copy(
            src_ref=part.at[b, i, pl.ds(0, half)], dst_ref=recv_b.at[b, i, pl.ds(0, half)],
            send_sem=b_send.at[b, i], recv_sem=b_recv.at[b, i],
            device_id=(me, other(1 << bits[i])), device_id_type=MESH,
        )

    def stage_c(b):
        half = rows_of(b) // 2
        rows = pl.ds(pl.multiple_of(core * half, 8), half)
        return pltpu.make_async_remote_copy(
            src_ref=fin.at[b, rows], dst_ref=fin.at[b, rows],
            send_sem=c_send.at[b], recv_sem=c_recv.at[b],
            device_id=(me, other(1)), device_id_type=MESH,
        )

    def after_a(b):
        half = rows_of(b) // 2
        stage_a(b).wait()
        value = g[b, pl.ds(pl.multiple_of(core * half, 8), half), :] + recv_a[b, 0:half, :]
        if bits:
            part[b, 0, 0:half, :] = value
            stage_b(b, 0).start()
        else:
            fin[b, pl.ds(pl.multiple_of(core * half, 8), half), :] = value
            stage_c(b).start()

    def after_b(b, i):
        half = rows_of(b) // 2
        stage_b(b, i).wait()
        value = part[b, i, 0:half, :] + recv_b[b, i, 0:half, :]
        if i + 1 < len(bits):
            part[b, i + 1, 0:half, :] = value
            stage_b(b, i + 1).start()
        else:
            fin[b, pl.ds(pl.multiple_of(core * half, 8), half), :] = value
            stage_c(b).start()

    steps = []
    for b in range(layers):
        steps.append([functools.partial(after_a, b)] + [functools.partial(after_b, b, i) for i in range(len(bits))])

    for b in range(layers):
        l = layers - 1 - b
        slot = b % 2
        dz_hi, dz_lo = dh[slot], dl[slot]
        lh = hh[l]
        grad = mm_nt(lh, dz_hi) + mm_nt(lh, dz_lo) + mm_nt(hl[l], dz_hi)
        bias_row = mm_nt(ones, dz_hi) + mm_nt(ones, dz_lo)
        g[b, 0:hid, :] = grad
        g[layers - 1, small + 4 + l:small + 5 + l, :] = bias_row[0:1]
        stage_a(b).start()
        for earlier in range(b):
            if steps[earlier]:
                steps[earlier].pop(0)()
        if l > 0:
            def back(at, l=l, slot=slot):
                lanes = pl.ds(at, chunk)
                hi = dh[slot, :, lanes]
                d = mm(wn[l - 1, 0], hi) + mm(wn[l - 1, 1], hi) + mm(wn[l - 1, 0], dl[slot, :, lanes])
                hi, lo = split(d * sg[l - 1, :, lanes])
                dh[1 - slot, :, lanes] = hi
                dl[1 - slot, :, lanes] = lo
            chunks(back)
            if steps[b]:
                steps[b].pop(0)()
    while any(steps):
        for b in range(layers):
            if steps[b]:
                steps[b].pop(0)()
    for b in range(layers):
        stage_c(b).wait()
        l = layers - 1 - b
        if l > 0:
            gmid_ref[0, l - 1] = fin[b, 0:hid, :]
        else:
            gin_ref[0] = fin[b, 0:hid, :]
    tail = fin[layers - 1, small:small + 16, :]
    gout_ref[0] = tail[0:4]
    ghid_ref[0] = tail[4:4 + layers]
    gbout_ref[...] = tail[7:8, 0:4]


def solution(mesh):
    slabs, n_rays = mesh.shape["slab"], mesh.shape["rays"]

    def shards(geometry, entry, counts, targets, w_in, w_mid, w_out, b_hid, b_out, freqs):
        width = geometry.shape[2]
        own = targets.shape[2]
        n = SAMP * width
        hid = w_in.shape[2]
        mid = w_mid.shape[1]
        layers = mid + 1
        delta = 3.0 / (SAMP * slabs)
        factor = 1.0 / math.sqrt(3.0 * n_rays * slabs * own)
        more = max(1, sum(1 for b in range(1, 16) if (1 << b) < n_rays))
        half = (hid + 16) // 2
        shape = jax.ShapeDtypeStruct
        return pl.pallas_call(
            functools.partial(kernel, slabs, n_rays, delta, factor),
            out_shape=(
                shape((3, 1, own), F32),
                shape((1, 2 * freqs.shape[2], hid), F32),
                shape((1, mid, hid, hid), F32),
                shape((1, 4, hid), F32),
                shape((1, layers, hid), F32),
                shape((1, 4), F32),
            ),
            in_specs=[pl.BlockSpec(memory_space=pltpu.VMEM)] * 10,
            out_specs=tuple([pl.BlockSpec(memory_space=pltpu.VMEM)] * 6),
            scratch_shapes=[
                pltpu.VMEM((layers + 1, hid, n), BF16),
                pltpu.VMEM((layers + 1, hid, n), BF16),
                pltpu.VMEM((layers, hid, n), F32),
                pltpu.VMEM((2, hid, n), BF16),
                pltpu.VMEM((2, hid, n), BF16),
                pltpu.VMEM((layers, 2, hid, hid), BF16),
                pltpu.VMEM((mid, 2, hid, hid), BF16),
                pltpu.VMEM((slabs, 8, width), F32),
                pltpu.VMEM((layers, hid + 16, hid), F32),
                pltpu.VMEM((layers, half, hid), F32),
                pltpu.VMEM((layers, more, half, hid), F32),
                pltpu.VMEM((layers, more, half, hid), F32),
                pltpu.VMEM((layers, hid + 16, hid), F32),
                pltpu.SemaphoreType.DMA((slabs,)),
                pltpu.SemaphoreType.DMA((slabs,)),
                pltpu.SemaphoreType.DMA((layers,)),
                pltpu.SemaphoreType.DMA((layers,)),
                pltpu.SemaphoreType.DMA((layers, more)),
                pltpu.SemaphoreType.DMA((layers, more)),
                pltpu.SemaphoreType.DMA((layers,)),
                pltpu.SemaphoreType.DMA((layers,)),
            ],
            compiler_params=pltpu.CompilerParams(
                collective_id=0, has_side_effects=True, vmem_limit_bytes=60 * 1024 * 1024
            ),
        )(geometry, entry, counts, targets, w_in, w_mid, w_out, b_hid, b_out, freqs)

    in_specs = (
        P(None, "rays", None),
        P("slab", "rays", None),
        P("slab", "rays", None),
        P(None, "rays", "slab"),
        P("slab", None, None),
        P("slab", None, None, None),
        P("slab", None, None),
        P("slab", None, None),
        P("slab", None),
        P("slab", None, None),
    )
    out_specs = (
        P(None, "rays", "slab"),
        P("slab", None, None),
        P("slab", None, None, None),
        P("slab", None, None),
        P("slab", None, None),
        P("slab", None),
    )
    return jax.shard_map(shards, mesh=mesh, in_specs=in_specs, out_specs=out_specs, check_vma=False)
```

time: 107 us -> 41.5 us (0.39)
  waiting for transfers between devices: 36.9 us -> 0 us
  Pallas kernels: 0 us -> 32.6 us
  matrix products: 25.1 us -> 0 us
  between operations: 14.4 us -> 0.66 us
  starting transfers between devices: 10.9 us -> 0 us
  blocking collectives: 6.95 us -> 0 us
  local copies, waits for them, and re-layouts: 11.1 us -> 8.02 us
  other arithmetic: 1.54 us -> 0 us
    pallas_call x0 -> x1, Pallas kernels: none -> 32.6 us  [shards(): pl.pallas_call(functools.partial(kernel, slabs, n_rays, delta, factor), o...]
    dot_general x12 -> x0, matrix products: 25.1 us -> none  [the longest x8 14.3 us: hidden_layer(): return jax.nn.softplus(jnp.dot(hidden, weight, precision=HIGH) + bias)]
    psum x1 -> x0, waiting for transfers between devices: 23.7 us -> none  [shards(): lax.psum((grads[0], grads[1], grads[2], grads[3], grads[4]), 'rays')]
    all_to_all x2 -> x0, waiting for transfers between devices: 13.2 us -> none  [the longest x1 6.88 us: shards(): lax.all_to_all(seg[:, None, :], 'slab', split_axis=2, concat_axis=1, tile...]
    all_to_all x2 -> x0, starting transfers between devices: 10.6 us -> none  [the longest x1 7.31 us: shards(): lax.all_to_all(seg[:, None, :], 'slab', split_axis=2, concat_axis=1, tile...]
    psum x1 -> x0, blocking collectives: 6.95 us -> none  [shards(): lax.psum((grads[0], grads[1], grads[2], grads[3], grads[4]), 'rays')]
    slice x5 -> x0, local copies, waits for them, and re-layouts: 1.93 us -> none  [the longest x1 1.84 us: composite(): logtrans = segments[3]]
    pallas_call x0 -> x1, local copies, waits for them, and re-layouts: none -> 1.32 us  [shards(): pl.pallas_call(functools.partial(kernel, slabs, n_rays, delta, factor), o...]
  transfers between devices with their start and end apart: 3 -> 0, of which waited for: 3 -> 0; matrix products, arithmetic and copies ran while one was open for 2% -> 0% of each run, Pallas kernels for 0% -> 0%
where the time goes in v1:
time: 41.5 us; the launch traced here: 41.3 us
  Pallas kernels  32.6 us (79%)
  local copies, waits for them, and re-layouts  8.02 us (19%)
  between operations  0.66 us (2%)
    pallas_call x1, Pallas kernels, shards(): pl.pallas_call(functools.partial(kernel, slabs, n_rays, delta, factor), o...  32.6 us
    unnamed x15, local copies, waits for them, and re-layouts  6.7 us
    pallas_call x1, local copies, waits for them, and re-layouts, shards(): pl.pallas_call(functools.partial(kernel, slabs, n_rays, delta, factor), o...  1.32 us

profile of v1, /device:TPU:0, one launch (start us, length us, event | category | flops | bytes accessed | tf_op | source)
XLA Modules:
  0.0 41.3 jit_solution(5911372070878738337)
XLA Ops:
  0.6 0.0 copy-start.2
  0.6 1.3 %copy.17.fr_ref = f32[1,3,128]{2,1,0:T(4,128)} copy(f32[1,3,128]{2,0,1:T(1,128)} %param.19) | data formatting | bytes 3072 | tf_op args[9]
  1.9 0.0 copy-done.2
  1.9 0.6 %copy.16.bhid_ref = f32[1,3,256]{2,1,0:T(4,128)} copy(f32[1,3,256]{2,0,1:T(1,128)S(1)} %copy-done.2) | data formatting | bytes 6144 | tf_op args[7]
  2.5 32.6 %shard_map.145 = (f32[3,1,16]{2,1,0:T(1,128)}, f32[1,256,256]{2,1,0:T(8,128)}, f32[1,2,256,256]{3,2,1,0:T(8,128)}, f32[1,4,256]{2,1,0:T(4,128)}, f32[1,3,256]{2,1,0:T(4,128)}, /*index=5*/f32[1,4]{1,0:T(1,128)}) custom-call(f32[6,1,128]{2,1,0:T(1,128)} %geo_ref.1, s32[1,1,128]{2,1,0:T(1,128)} %ent_ref.1, s32[1,1,128]{2,1,0:T(1,128)} %cnt_ref.1, ...), custom_call_target="tpu_custom_call" | custom-call | tf_op jit(solution)/shard_map/pallas_call | solution.py:371
  35.1 0.0 copy-start
  35.1 1.3 %copy.18 = f32[1,3,256]{2,0,1:T(1,128)} copy(f32[1,3,256]{2,1,0:T(4,128)} %get-tuple-element.10) | data formatting | bytes 6144 | tf_op jit(solution)/shard_map/pallas_call | solution.py:371
  36.5 1.2 %copy.24 = f32[3,1,16]{2,1,0:T(1,128)} copy(f32[3,1,16]{2,1,0:T(1,128)} %get-tuple-element.18) | data formatting | bytes 384
  37.7 1.7 %copy.25 = f32[1,256,256]{2,1,0:T(8,128)} copy(f32[1,256,256]{2,1,0:T(8,128)} %get-tuple-element.19) | data formatting | bytes 524288
  39.4 0.0 copy-done
  39.4 0.0 copy-start.1
  39.4 0.8 %copy.26 = f32[1,2,256,256]{3,2,1,0:T(8,128)} copy(f32[1,2,256,256]{3,2,1,0:T(8,128)S(1)} %copy-done) | data formatting | bytes 1048576
  40.2 0.0 copy-done.1
  40.2 0.0 copy-start.3
  40.2 0.6 %copy.27 = f32[1,4,256]{2,1,0:T(4,128)} copy(f32[1,4,256]{2,1,0:T(4,128)S(1)} %copy-done.1) | data formatting | bytes 8192
  40.8 0.0 copy-done.3
  40.8 0.5 %copy.28 = f32[1,4]{1,0:T(1,128)} copy(f32[1,4]{1,0:T(1,128)S(1)} %copy-done.3) | data formatting | bytes 32
Async XLA Ops:
  0.6 1.3 %copy-start.2 = (f32[1,3,256]{2,0,1:T(1,128)S(1)}, f32[1,3,256]{2,0,1:T(1,128)}, u32[]{:S(2)}) copy-start(f32[1,3,256]{2,0,1:T(1,128)} %param.17) | copy-start | bytes 9220
  35.1 4.2 %copy-start = (f32[1,2,256,256]{3,2,1,0:T(8,128)S(1)}, f32[1,2,256,256]{3,2,1,0:T(8,128)}, u32[]{:S(2)}) copy-start(f32[1,2,256,256]{3,2,1,0:T(8,128)} %get-tuple-element.20) | copy-start | bytes 1572868
  39.4 0.8 %copy-start.1 = (f32[1,4,256]{2,1,0:T(4,128)S(1)}, f32[1,4,256]{2,1,0:T(4,128)}, u32[]{:S(2)}) copy-start(f32[1,4,256]{2,1,0:T(4,128)} %get-tuple-element.21) | copy-start | bytes 12292
  40.2 0.6 %copy-start.3 = (f32[1,4]{1,0:T(1,128)S(1)}, f32[1,4]{1,0:T(1,128)}, u32[]{:S(2)}) copy-start(f32[1,4]{1,0:T(1,128)} %get-tuple-element.23) | copy-start | bytes 52

commit v2 on v1

--- a/solution.py
+++ b/solution.py
@@ -51,11 +51,15 @@
 
 def kernel(
     slabs, n_rays, delta, factor,
-    geo_ref, ent_ref, cnt_ref, tgt_ref, win_ref, wmid_ref, wout_ref, bhid_ref, bout_ref, fr_ref,
-    pix_ref, gin_ref, gmid_ref, gout_ref, ghid_ref, gbout_ref,
-    hh, hl, sg, dh, dl, wt, wn, seg_all, g, recv_a, recv_b, part, fin,
-    seg_send, seg_recv, a_send, a_recv, b_send, b_recv, c_send, c_recv,
+    *refs,
 ):
+    far, (pix_ref, fin), near = refs[:10], refs[10:12], refs[12:22]
+    geo_ref, ent_ref, cnt_ref, tgt_ref, win_ref, wmid_ref, wout_ref, bhid_ref, bout_ref, fr_ref = near
+    hh, hl, sg, dh, dl, wt, wn, seg_all, g, recv_a, recv_b, part = refs[22:34]
+    load_sem, seg_send, seg_recv, a_send, a_recv, b_send, b_recv, c_send, c_recv = refs[34:]
+    loads = [pltpu.make_async_copy(far[i], near[i], load_sem.at[i]) for i in range(10)]
+    for i in (0, 1, 9, 4, 7, 5, 6, 8, 2, 3):
+        loads[i].start()
     me = lax.axis_index("slab")
     ray = lax.axis_index("rays")
     core = lax.rem(ray, 2)
@@ -92,19 +96,9 @@
                 return carry
             lax.fori_loop(0, n_chunks, step, 0)
 
-    for l in range(layers):
-        w = win_ref[0] if l == 0 else wmid_ref[0, l - 1]
-        hi, lo = split(w.T)
-        wt[l, 0] = hi
-        wt[l, 1] = lo
-        if l > 0:
-            hi, lo = split(w)
-            wn[l - 1, 0] = hi
-            wn[l - 1, 1] = lo
-
-    pad5 = jnp.zeros((8 - layers, hid), F32)
-    bias = jnp.concatenate([bhid_ref[0], pad5], axis=0).T
-    freq = jnp.concatenate([fr_ref[0], jnp.zeros((5, fe), F32)], axis=0).T
+    for i in (0, 1, 9):
+        loads[i].wait()
+    freq = jnp.concatenate([fr_ref[:, 0, :], jnp.zeros((5, fe), F32)], axis=0).T
 
     geo = geo_ref[:, 0, :]
     t0 = 0.25 * (ent_ref[0].astype(F32) + 0.5)
@@ -127,6 +121,21 @@
         hl[0, fe:2 * fe, lanes] = lo
         if j < SAMP - 1:
             sn, cs = sn * cd + cs * sd, cs * cd - sn * sd
+
+    for i in (2, 3, 4, 5, 6, 7, 8):
+        loads[i].wait()
+    for l in range(layers):
+        w = win_ref[0] if l == 0 else wmid_ref[0, l - 1]
+        hi, lo = split(w.T)
+        wt[l, 0] = hi
+        wt[l, 1] = lo
+        if l > 0:
+            hi, lo = split(w)
+            wn[l - 1, 0] = hi
+            wn[l - 1, 1] = lo
+
+    pad5 = jnp.zeros((8 - layers, hid), F32)
+    bias = jnp.concatenate([bhid_ref[:, 0, :], pad5], axis=0).T
 
     for l in range(layers):
         def layer(at, l=l):
@@ -213,7 +222,7 @@
         term = shades[s] * jnp.sum(pull * colors[s], axis=0, keepdims=True)
         d_log = d_log + jnp.where(me < s, term, 0.0)
     d_color = mine_shade * pull
-    pix_ref[:, 0, :] = lax.dot_general(
+    pix_ref[...] = lax.dot_general(
         pixels, spread, NT, precision=lax.Precision.HIGHEST, preferred_element_type=F32
     )
 
@@ -342,15 +351,24 @@
                 steps[b].pop(0)()
     for b in range(layers):
         stage_c(b).wait()
-        l = layers - 1 - b
-        if l > 0:
-            gmid_ref[0, l - 1] = fin[b, 0:hid, :]
-        else:
-            gin_ref[0] = fin[b, 0:hid, :]
-    tail = fin[layers - 1, small:small + 16, :]
+
+
+def unpack(pix_in, fin, pix_ref, gin_ref, gmid_ref, gout_ref, ghid_ref, gbout_ref, sems):
+    layers = fin.shape[0]
+    hid = fin.shape[2]
+    copies = []
+    for l in range(layers):
+        place = gin_ref.at[0] if l == 0 else gmid_ref.at[0, l - 1]
+        copies.append(pltpu.make_async_copy(fin.at[layers - 1 - l, pl.ds(0, hid)], place, sems.at[l]))
+    for copy in copies:
+        copy.start()
+    tail = fin[layers - 1, hid:hid + 16, :]
     gout_ref[0] = tail[0:4]
-    ghid_ref[0] = tail[4:4 + layers]
+    ghid_ref[:, 0, :] = tail[4:4 + layers]
     gbout_ref[...] = tail[7:8, 0:4]
+    pix_ref[:, 0, :] = pix_in[0:3, :]
+    for copy in copies:
+        copy.wait()
 
 
 def solution(mesh):
@@ -368,19 +386,19 @@
         more = max(1, sum(1 for b in range(1, 16) if (1 << b) < n_rays))
         half = (hid + 16) // 2
         shape = jax.ShapeDtypeStruct
-        return pl.pallas_call(
+        args = (
+            geometry, entry, counts, targets, w_in, w_mid, w_out,
+            jnp.transpose(b_hid, (1, 0, 2)), b_out, jnp.transpose(freqs, (1, 0, 2)),
+        )
+        vmem = pl.BlockSpec(memory_space=pltpu.VMEM)
+        item = 4 * hid * n
+        need = item * (2 * layers + 4) + item * layers + 16 * (1 << 20) + 64 * slabs * width
+        pixels, packed = pl.pallas_call(
             functools.partial(kernel, slabs, n_rays, delta, factor),
-            out_shape=(
-                shape((3, 1, own), F32),
-                shape((1, 2 * freqs.shape[2], hid), F32),
-                shape((1, mid, hid, hid), F32),
-                shape((1, 4, hid), F32),
-                shape((1, layers, hid), F32),
-                shape((1, 4), F32),
-            ),
-            in_specs=[pl.BlockSpec(memory_space=pltpu.VMEM)] * 10,
-            out_specs=tuple([pl.BlockSpec(memory_space=pltpu.VMEM)] * 6),
-            scratch_shapes=[
+            out_shape=(shape((3, own), F32), shape((layers, hid + 16, hid), F32)),
+            in_specs=[pl.BlockSpec(memory_space=pltpu.HBM)] * 10,
+            out_specs=(vmem, vmem),
+            scratch_shapes=[pltpu.VMEM(a.shape, a.dtype) for a in args] + [
                 pltpu.VMEM((layers + 1, hid, n), BF16),
                 pltpu.VMEM((layers + 1, hid, n), BF16),
                 pltpu.VMEM((layers, hid, n), F32),
@@ -393,7 +411,7 @@
                 pltpu.VMEM((layers, half, hid), F32),
                 pltpu.VMEM((layers, more, half, hid), F32),
                 pltpu.VMEM((layers, more, half, hid), F32),
-                pltpu.VMEM((layers, hid + 16, hid), F32),
+                pltpu.SemaphoreType.DMA((10,)),
                 pltpu.SemaphoreType.DMA((slabs,)),
                 pltpu.SemaphoreType.DMA((slabs,)),
                 pltpu.SemaphoreType.DMA((layers,)),
@@ -404,9 +422,26 @@
                 pltpu.SemaphoreType.DMA((layers,)),
             ],
             compiler_params=pltpu.CompilerParams(
-                collective_id=0, has_side_effects=True, vmem_limit_bytes=60 * 1024 * 1024
+                collective_id=0, has_side_effects=True, vmem_limit_bytes=min(need, 60 << 20)
             ),
-        )(geometry, entry, counts, targets, w_in, w_mid, w_out, b_hid, b_out, freqs)
+        )(*args)
+        hbm = pl.BlockSpec(memory_space=pltpu.HBM)
+        outs = pl.pallas_call(
+            unpack,
+            out_shape=(
+                shape((3, 1, own), F32),
+                shape((1, 2 * freqs.shape[2], hid), F32),
+                shape((1, mid, hid, hid), F32),
+                shape((1, 4, hid), F32),
+                shape((layers, 1, hid), F32),
+                shape((1, 4), F32),
+            ),
+            in_specs=[vmem] * 2,
+            out_specs=(vmem, hbm, hbm, vmem, vmem, vmem),
+            scratch_shapes=[pltpu.SemaphoreType.DMA((layers,))],
+            compiler_params=pltpu.CompilerParams(vmem_limit_bytes=8 << 20),
+        )(pixels, packed)
+        return outs[:4] + (jnp.transpose(outs[4], (1, 0, 2)), outs[5])
 
     in_specs = (
         P(None, "rays", None),

time: 41.5 us -> 40 us (0.964)
  local copies, waits for them, and re-layouts: 8.02 us -> 6.7 us
    pallas_call x1, Pallas kernels: 32.6 us -> 30.7 us  [shards(): pl.pallas_call(functools.partial(kernel, slabs, n_rays, delta, factor), o...]
    pallas_call x0 -> x1, Pallas kernels: none -> 1.5 us  [shards(): pl.pallas_call(unpack, out_shape=(shape((3, 1, own), F32), shape((1, 2 *...]
    pallas_call x1 -> x0, local copies, waits for them, and re-layouts: 1.32 us -> none  [shards(): pl.pallas_call(functools.partial(kernel, slabs, n_rays, delta, factor), o...]
    unnamed x15 -> x20, local copies, waits for them, and re-layouts: 6.7 us -> 6.7 us
where the time goes in v2:
time: 40 us; the launch traced here: 39.6 us
  Pallas kernels  32.2 us (81%)
  local copies, waits for them, and re-layouts  6.7 us (17%)
  between operations  0.67 us (2%)
    pallas_call x1, Pallas kernels, shards(): pl.pallas_call(functools.partial(kernel, slabs, n_rays, delta, factor), o...  30.7 us
    unnamed x20, local copies, waits for them, and re-layouts  6.7 us
    pallas_call x1, Pallas kernels, shards(): pl.pallas_call(unpack, out_shape=(shape((3, 1, own), F32), shape((1, 2 *...  1.5 us

profile of v2, /device:TPU:0, one launch (start us, length us, event | category | flops | bytes accessed | tf_op | source)
XLA Modules:
  0.0 39.6 jit_solution(6266542964016861745)
XLA Ops:
  0.6 0.0 copy-start.3
  0.6 0.0 copy-start.7
  0.7 0.7 %copy-done.3 = f32[6,1,128]{2,1,0:T(1,128)S(1)} copy-done((f32[6,1,128]{2,1,0:T(1,128)S(1)}, f32[6,1,128]{2,1,0:T(1,128)}, u32[]{:S(2)}) %copy-start.3) | copy-done | bytes 3096
  1.3 0.0 copy-done.7
  1.3 0.0 copy-start
  1.3 1.0 %copy-done = f32[1,2,256,256]{3,2,1,0:T(8,128)S(1)} copy-done((f32[1,2,256,256]{3,2,1,0:T(8,128)S(1)}, f32[1,2,256,256]{3,2,1,0:T(8,128)}, u32[]{:S(2)}) %copy-start) | copy-done | bytes 524312
  2.4 0.0 copy-start.1
  2.4 0.9 %copy-done.1 = f32[1,256,256]{2,1,0:T(8,128)S(1)} copy-done((f32[1,256,256]{2,1,0:T(8,128)S(1)}, f32[1,256,256]{2,1,0:T(8,128)}, u32[]{:S(2)}) %copy-start.1) | copy-done | bytes 262168
  3.3 0.0 copy-start.2
  3.3 0.7 %copy-done.2 = f32[1,4,256]{2,1,0:T(4,128)S(1)} copy-done((f32[1,4,256]{2,1,0:T(4,128)S(1)}, f32[1,4,256]{2,1,0:T(4,128)}, u32[]{:S(2)}) %copy-start.2) | copy-done | bytes 4120
  4.0 0.0 copy-start.4
  4.0 0.7 %copy-done.4 = f32[1,3,256]{2,0,1:T(1,128)S(1)} copy-done((f32[1,3,256]{2,0,1:T(1,128)S(1)}, f32[1,3,256]{2,0,1:T(1,128)}, u32[]{:S(2)}) %copy-start.4) | copy-done | bytes 3096
  4.7 0.0 copy-start.5
  4.7 0.7 %copy-done.5 = f32[3,1,16]{2,1,0:T(1,128)S(1)} copy-done((f32[3,1,16]{2,1,0:T(1,128)S(1)}, f32[3,1,16]{2,1,0:T(1,128)}, u32[]{:S(2)}) %copy-start.5) | copy-done | bytes 216
  5.4 0.0 copy-start.6
  5.4 0.7 %copy-done.6 = f32[1,3,128]{2,0,1:T(1,128)S(1)} copy-done((f32[1,3,128]{2,0,1:T(1,128)S(1)}, f32[1,3,128]{2,0,1:T(1,128)}, u32[]{:S(2)}) %copy-start.6) | copy-done | bytes 1560
  6.1 0.0 copy-start.8
  6.1 0.7 %copy-done.8 = s32[1,1,128]{2,1,0:T(1,128)S(1)} copy-done((s32[1,1,128]{2,1,0:T(1,128)S(1)}, s32[1,1,128]{2,1,0:T(1,128)}, u32[]{:S(2)}) %copy-start.8) | copy-done | bytes 536
  6.7 0.0 copy-start.9
  6.7 0.7 %copy-done.9 = f32[1,4]{1,0:T(1,128)S(1)} copy-done((f32[1,4]{1,0:T(1,128)S(1)}, f32[1,4]{1,0:T(1,128)}, u32[]{:S(2)}) %copy-start.9) | copy-done | bytes 40
  7.4 30.7 %shard_map.145 = (f32[3,16]{1,0:T(4,128)S(1)}, f32[3,272,256]{2,1,0:T(8,128)S(1)}) custom-call(f32[6,1,128]{2,1,0:T(1,128)S(1)} %copy-done.3, s32[1,1,128]{2,1,0:T(1,128)S(1)} %copy-done.7, s32[1,1,128]{2,1,0:T(1,128)S(1)} %copy-done.8, f32[3,1,16]{2,1,0:T(1,128)S(1)} %copy-done.5, f32[1,256,256]{2,1,0:T(8,128)S(1)} %copy-done.1, ...), custom_call_target="tpu_custom_call" | custom-call | tf_op jit(solution)/shard_map/pallas_call | solution.py:396
  38.1 1.5 %shard_map.146 = (f32[3,1,16]{2,1,0:T(1,128)}, f32[1,256,256]{2,1,0:T(8,128)}, f32[1,2,256,256]{3,2,1,0:T(8,128)}, f32[1,4,256]{2,1,0:T(4,128)}, f32[3,1,256]{2,1,0:T(1,128)}, /*index=5*/f32[1,4]{1,0:T(1,128)}) custom-call(f32[3,16]{1,0:T(4,128)S(1)} %get-tuple-element.14.pix_in, f32[3,272,256]{2,1,0:T(8,128)S(1)} %get-tuple-element.15.fin), custom_call_target="tpu_custom_call" | custom-call | tf_op jit(solution)/shard_map/pallas_call | solution.py:429
Async XLA Ops:
  0.6 0.7 %copy-start.3 = (f32[6,1,128]{2,1,0:T(1,128)S(1)}, f32[6,1,128]{2,1,0:T(1,128)}, u32[]{:S(2)}) copy-start(f32[6,1,128]{2,1,0:T(1,128)} %refs_0_.1) | copy-start | bytes 9220
  0.6 0.7 %copy-start.7 = (s32[1,1,128]{2,1,0:T(1,128)S(1)}, s32[1,1,128]{2,1,0:T(1,128)}, u32[]{:S(2)}) copy-start(s32[1,1,128]{2,1,0:T(1,128)} %refs_1_.1) | copy-start | bytes 1540
  1.3 1.0 %copy-start = (f32[1,2,256,256]{3,2,1,0:T(8,128)S(1)}, f32[1,2,256,256]{3,2,1,0:T(8,128)}, u32[]{:S(2)}) copy-start(f32[1,2,256,256]{3,2,1,0:T(8,128)} %refs_5_.1) | copy-start | bytes 1572868
  2.4 0.9 %copy-start.1 = (f32[1,256,256]{2,1,0:T(8,128)S(1)}, f32[1,256,256]{2,1,0:T(8,128)}, u32[]{:S(2)}) copy-start(f32[1,256,256]{2,1,0:T(8,128)} %refs_4_.1) | copy-start | bytes 786436
  3.3 0.7 %copy-start.2 = (f32[1,4,256]{2,1,0:T(4,128)S(1)}, f32[1,4,256]{2,1,0:T(4,128)}, u32[]{:S(2)}) copy-start(f32[1,4,256]{2,1,0:T(4,128)} %refs_6_.1) | copy-start | bytes 12292
  4.0 0.7 %copy-start.4 = (f32[1,3,256]{2,0,1:T(1,128)S(1)}, f32[1,3,256]{2,0,1:T(1,128)}, u32[]{:S(2)}) copy-start(f32[1,3,256]{2,0,1:T(1,128)} %param.17) | copy-start | bytes 9220
  4.7 0.7 %copy-start.5 = (f32[3,1,16]{2,1,0:T(1,128)S(1)}, f32[3,1,16]{2,1,0:T(1,128)}, u32[]{:S(2)}) copy-start(f32[3,1,16]{2,1,0:T(1,128)} %refs_3_.1) | copy-start | bytes 580
  5.4 0.7 %copy-start.6 = (f32[1,3,128]{2,0,1:T(1,128)S(1)}, f32[1,3,128]{2,0,1:T(1,128)}, u32[]{:S(2)}) copy-start(f32[1,3,128]{2,0,1:T(1,128)} %param.19) | copy-start | bytes 4612
  6.1 0.7 %copy-start.8 = (s32[1,1,128]{2,1,0:T(1,128)S(1)}, s32[1,1,128]{2,1,0:T(1,128)}, u32[]{:S(2)}) copy-start(s32[1,1,128]{2,1,0:T(1,128)} %refs_2_.1) | copy-start | bytes 1540
  6.7 0.7 %copy-start.9 = (f32[1,4]{1,0:T(1,128)S(1)}, f32[1,4]{1,0:T(1,128)}, u32[]{:S(2)}) copy-start(f32[1,4]{1,0:T(1,128)} %refs_8_.1) | copy-start | bytes 52

commit v3 on v2

--- a/solution.py
+++ b/solution.py
@@ -55,8 +55,8 @@
 ):
     far, (pix_ref, fin), near = refs[:10], refs[10:12], refs[12:22]
     geo_ref, ent_ref, cnt_ref, tgt_ref, win_ref, wmid_ref, wout_ref, bhid_ref, bout_ref, fr_ref = near
-    hh, hl, sg, dh, dl, wt, wn, seg_all, g, recv_a, recv_b, part = refs[22:34]
-    load_sem, seg_send, seg_recv, a_send, a_recv, b_send, b_recv, c_send, c_recv = refs[34:]
+    hx, sg, dh, dl, wt, wn, seg_all, g, recv_a, recv_b, part = refs[22:33]
+    load_sem, seg_send, seg_recv, a_send, a_recv, b_send, b_recv, c_send, c_recv = refs[33:]
     loads = [pltpu.make_async_copy(far[i], near[i], load_sem.at[i]) for i in range(10)]
     for i in (0, 1, 9, 4, 7, 5, 6, 8, 2, 3):
         loads[i].start()
@@ -114,25 +114,26 @@
     for j in range(SAMP):
         lanes = slice(j * width, (j + 1) * width)
         hi, lo = split(sn)
-        hh[0, 0:fe, lanes] = hi
-        hl[0, 0:fe, lanes] = lo
+        hx[0, hid:hid + fe, lanes] = hi
+        hx[0, 0:fe, lanes] = lo
         hi, lo = split(cs)
-        hh[0, fe:2 * fe, lanes] = hi
-        hl[0, fe:2 * fe, lanes] = lo
+        hx[0, hid + fe:hid + 2 * fe, lanes] = hi
+        hx[0, fe:2 * fe, lanes] = lo
         if j < SAMP - 1:
             sn, cs = sn * cd + cs * sd, cs * cd - sn * sd
 
     for i in (2, 3, 4, 5, 6, 7, 8):
         loads[i].wait()
     for l in range(layers):
+        hx[l, 2 * hid:2 * hid + 16, :] = jnp.ones((16, n), BF16)
         w = win_ref[0] if l == 0 else wmid_ref[0, l - 1]
         hi, lo = split(w.T)
-        wt[l, 0] = hi
-        wt[l, 1] = lo
+        wt[l, 0:hid] = hi
+        wt[l, hid:2 * hid] = lo
         if l > 0:
             hi, lo = split(w)
-            wn[l - 1, 0] = hi
-            wn[l - 1, 1] = lo
+            wn[l - 1, 0:hid] = hi
+            wn[l - 1, hid:2 * hid] = lo
 
     pad5 = jnp.zeros((8 - layers, hid), F32)
     bias = jnp.concatenate([bhid_ref[:, 0, :], pad5], axis=0).T
@@ -140,20 +141,20 @@
     for l in range(layers):
         def layer(at, l=l):
             lanes = pl.ds(at, chunk)
-            hi = hh[l, :, lanes]
-            z = mm(wt[l, 0], hi) + mm(wt[l, 1], hi) + mm(wt[l, 0], hl[l, :, lanes])
+            both = mm(wt[l], hx[l, hid:2 * hid, lanes])
+            z = both[0:hid] + both[hid:2 * hid] + mm(wt[l, 0:hid], hx[l, 0:hid, lanes])
             z = z + bias[:, l:l + 1]
             h = softplus(z)
             sg[l, :, lanes] = jnp.exp(z - h)
             hi, lo = split(h)
-            hh[l + 1, :, lanes] = hi
-            hl[l + 1, :, lanes] = lo
+            hx[l + 1, hid:2 * hid, lanes] = hi
+            hx[l + 1, 0:hid, lanes] = lo
         chunks(layer)
 
     wo = jnp.concatenate([wout_ref[0], jnp.zeros((4, hid), F32)], axis=0)
     wo_hi, wo_lo = split(wo)
-    last_hi = hh[layers]
-    out = mm(wo_hi, last_hi) + mm(wo_lo, last_hi) + mm(wo_hi, hl[layers])
+    pair = mm(jnp.concatenate([wo_hi, wo_lo], axis=0), hx[layers, hid:2 * hid, :])
+    out = pair[0:8] + pair[8:16] + mm(wo_hi, hx[layers, 0:hid, :])
     bout = jnp.concatenate([bout_ref[...], jnp.zeros((7, 4), F32)], axis=0)
     counts = cnt_ref[0]
     sigma = softplus(out[0:1] + bout[0:1, 0:1])
@@ -242,8 +243,8 @@
 
     def last(at):
         lanes = pl.ds(at, chunk)
-        hi, lo = (d_hi_ref(at), d_lo_ref(at))
-        d = mm(wot_hi, hi) + mm(wot_lo, hi) + mm(wot_hi, lo)
+        hi = dh[1, 0:8, lanes]
+        d = mm(wot_hi, hi) + mm(wot_lo, hi) + mm(wot_hi, dl[1, 0:8, lanes])
         hi, lo = split(d * sg[layers - 1, :, lanes])
         dh[0, :, lanes] = hi
         dl[0, :, lanes] = lo
@@ -251,17 +252,12 @@
     dh[1, 0:8, :] = do_hi
     dl[1, 0:8, :] = do_lo
 
-    def d_hi_ref(at):
-        return dh[1, 0:8, pl.ds(at, chunk)]
-
-    def d_lo_ref(at):
-        return dl[1, 0:8, pl.ds(at, chunk)]
-
     small = hid
-    ones = jnp.ones((16, n), BF16)
     g[layers - 1, small:small + 16, :] = jnp.zeros((16, hid), F32)
-    g_out = mm_nt(do_hi, last_hi) + mm_nt(do_lo, last_hi) + mm_nt(do_hi, hl[layers])
+    pair = mm_nt(jnp.concatenate([do_hi, do_lo], axis=0), hx[layers, hid:2 * hid, :])
+    g_out = pair[0:8] + pair[8:16] + mm_nt(do_hi, hx[layers, 0:hid, :])
     g[layers - 1, small:small + 4, :] = g_out[0:4]
+    ones = hx[0, 2 * hid:2 * hid + 16, :]
     row = mm_nt(ones, do_hi) + mm_nt(ones, do_lo)
     g[layers - 1, small + 7:small + 8, 0:8] = row[0:1, 0:8]
     chunks(last)
@@ -325,10 +321,10 @@
         l = layers - 1 - b
         slot = b % 2
         dz_hi, dz_lo = dh[slot], dl[slot]
-        lh = hh[l]
-        grad = mm_nt(lh, dz_hi) + mm_nt(lh, dz_lo) + mm_nt(hl[l], dz_hi)
-        bias_row = mm_nt(ones, dz_hi) + mm_nt(ones, dz_lo)
-        g[b, 0:hid, :] = grad
+        first = mm_nt(hx[l], dz_hi)
+        second = mm_nt(hx[l, hid:2 * hid + 16], dz_lo)
+        bias_row = first[2 * hid:2 * hid + 16] + second[hid:hid + 16]
+        g[b, 0:hid, :] = first[0:hid] + first[hid:2 * hid] + second[0:hid]
         g[layers - 1, small + 4 + l:small + 5 + l, :] = bias_row[0:1]
         stage_a(b).start()
         for earlier in range(b):
@@ -337,8 +333,8 @@
         if l > 0:
             def back(at, l=l, slot=slot):
                 lanes = pl.ds(at, chunk)
-                hi = dh[slot, :, lanes]
-                d = mm(wn[l - 1, 0], hi) + mm(wn[l - 1, 1], hi) + mm(wn[l - 1, 0], dl[slot, :, lanes])
+                both = mm(wn[l - 1], dh[slot, :, lanes])
+                d = both[0:hid] + both[hid:2 * hid] + mm(wn[l - 1, 0:hid], dl[slot, :, lanes])
                 hi, lo = split(d * sg[l - 1, :, lanes])
                 dh[1 - slot, :, lanes] = hi
                 dl[1 - slot, :, lanes] = lo
@@ -391,21 +387,18 @@
             jnp.transpose(b_hid, (1, 0, 2)), b_out, jnp.transpose(freqs, (1, 0, 2)),
         )
         vmem = pl.BlockSpec(memory_space=pltpu.VMEM)
-        item = 4 * hid * n
-        need = item * (2 * layers + 4) + item * layers + 16 * (1 << 20) + 64 * slabs * width
         pixels, packed = pl.pallas_call(
             functools.partial(kernel, slabs, n_rays, delta, factor),
-            out_shape=(shape((3, own), F32), shape((layers, hid + 16, hid), F32)),
+            out_shape=(pltpu.VMEM((3, own), F32), pltpu.VMEM((layers, hid + 16, hid), F32)),
             in_specs=[pl.BlockSpec(memory_space=pltpu.HBM)] * 10,
             out_specs=(vmem, vmem),
             scratch_shapes=[pltpu.VMEM(a.shape, a.dtype) for a in args] + [
-                pltpu.VMEM((layers + 1, hid, n), BF16),
-                pltpu.VMEM((layers + 1, hid, n), BF16),
+                pltpu.VMEM((layers + 1, 2 * hid + 16, n), BF16),
                 pltpu.VMEM((layers, hid, n), F32),
                 pltpu.VMEM((2, hid, n), BF16),
                 pltpu.VMEM((2, hid, n), BF16),
-                pltpu.VMEM((layers, 2, hid, hid), BF16),
-                pltpu.VMEM((mid, 2, hid, hid), BF16),
+                pltpu.VMEM((layers, 2 * hid, hid), BF16),
+                pltpu.VMEM((mid, 2 * hid, hid), BF16),
                 pltpu.VMEM((slabs, 8, width), F32),
                 pltpu.VMEM((layers, hid + 16, hid), F32),
                 pltpu.VMEM((layers, half, hid), F32),
@@ -422,7 +415,7 @@
                 pltpu.SemaphoreType.DMA((layers,)),
             ],
             compiler_params=pltpu.CompilerParams(
-                collective_id=0, has_side_effects=True, vmem_limit_bytes=min(need, 60 << 20)
+                collective_id=0, has_side_effects=True, vmem_limit_bytes=58 * 1000 * 1024
             ),
         )(*args)
         hbm = pl.BlockSpec(memory_space=pltpu.HBM)

time: 40 us -> 33.8 us (0.84)
  local copies, waits for them, and re-layouts: 6.7 us -> 0 us
  Pallas kernels: 32.2 us -> 33 us
    unnamed x20 -> x0, local copies, waits for them, and re-layouts: 6.7 us -> none
    pallas_call x1, Pallas kernels: 30.7 us -> 31.5 us  [shards(): pl.pallas_call(functools.partial(kernel, slabs, n_rays, delta, factor), o...]
where the time goes in v3:
time: 33.8 us; the launch traced here: 33.7 us
  Pallas kernels  33 us (98%)
  between operations  0.64 us (2%)
    pallas_call x1, Pallas kernels, shards(): pl.pallas_call(functools.partial(kernel, slabs, n_rays, delta, factor), o...  31.5 us
    pallas_call x1, Pallas kernels, shards(): pl.pallas_call(unpack, out_shape=(shape((3, 1, own), F32), shape((1, 2 *...  1.5 us

profile of v3, /device:TPU:0, one launch (start us, length us, event | category | flops | bytes accessed | tf_op | source)
XLA Modules:
  0.0 33.7 jit_solution(7408340282569065904)
XLA Ops:
  0.6 31.5 %shard_map.145 = (f32[3,16]{1,0:T(4,128)S(1)}, f32[3,272,256]{2,1,0:T(8,128)S(1)}) custom-call(f32[6,1,128]{2,1,0:T(1,128)} %refs_0_.1, s32[1,1,128]{2,1,0:T(1,128)} %refs_1_.1, s32[1,1,128]{2,1,0:T(1,128)} %refs_2_.1, f32[3,1,16]{2,1,0:T(1,128)} %refs_3_.1, f32[1,256,256]{2,1,0:T(8,128)} %refs_4_.1, f32[1,2,256,256]{3,2,1,0:T(8,128)} %refs_5_.1, ...), custom_call_target="tpu_custom_call" | custom-call | tf_op jit(solution)/shard_map/pallas_call | solution.py:390
  32.2 1.5 %shard_map.146 = (f32[3,1,16]{2,1,0:T(1,128)}, f32[1,256,256]{2,1,0:T(8,128)}, f32[1,2,256,256]{3,2,1,0:T(8,128)}, f32[1,4,256]{2,1,0:T(4,128)}, f32[3,1,256]{2,1,0:T(1,128)}, /*index=5*/f32[1,4]{1,0:T(1,128)}) custom-call(f32[3,16]{1,0:T(4,128)S(1)} %get-tuple-element.14.pix_in, f32[3,272,256]{2,1,0:T(8,128)S(1)} %get-tuple-element.15.fin), custom_call_target="tpu_custom_call" | custom-call | tf_op jit(solution)/shard_map/pallas_call | solution.py:422

commit v4 on v3

--- a/solution.py
+++ b/solution.py
@@ -10,6 +10,7 @@
 
 SAMP = 8
 F32 = jnp.float32
+PIECES = 2
 BF16 = jnp.bfloat16
 MESH = pl.DeviceIdType.MESH
 NT = (((1,), (1,)), ((), ()))
@@ -253,65 +254,69 @@
     dl[1, 0:8, :] = do_lo
 
     small = hid
-    g[layers - 1, small:small + 16, :] = jnp.zeros((16, hid), F32)
-    pair = mm_nt(jnp.concatenate([do_hi, do_lo], axis=0), hx[layers, hid:2 * hid, :])
-    g_out = pair[0:8] + pair[8:16] + mm_nt(do_hi, hx[layers, 0:hid, :])
-    g[layers - 1, small:small + 4, :] = g_out[0:4]
-    ones = hx[0, 2 * hid:2 * hid + 16, :]
-    row = mm_nt(ones, do_hi) + mm_nt(ones, do_lo)
-    g[layers - 1, small + 7:small + 8, 0:8] = row[0:1, 0:8]
+    g[layers - 1, small:small + 32, :] = jnp.zeros((32, hid), F32)
+
+    def head_grads():
+        pair = mm_nt(jnp.concatenate([do_hi, do_lo], axis=0), hx[layers, hid:2 * hid, :])
+        g_out = pair[0:8] + pair[8:16] + mm_nt(do_hi, hx[layers, 0:hid, :])
+        g[layers - 1, small:small + 4, :] = g_out[0:4]
+        ones = hx[0, 2 * hid:2 * hid + 16, :]
+        row = mm_nt(ones, do_hi) + mm_nt(ones, do_lo)
+        g[layers - 1, small + 7:small + 8, 0:8] = row[0:1, 0:8]
+
     chunks(last)
 
     def rows_of(b):
-        return hid + 16 if b == layers - 1 else hid
-
-    def stage_a(b):
-        half = rows_of(b) // 2
+        return hid + 32 if b == layers - 1 else hid
+
+    def piece(b):
+        return rows_of(b) // 2 // PIECES
+
+    def at_core(b, p, which):
+        return pl.ds(pl.multiple_of(which * (rows_of(b) // 2) + p * piece(b), 8), piece(b))
+
+    def stage_a(b, p):
         return pltpu.make_async_remote_copy(
-            src_ref=g.at[b, pl.ds(pl.multiple_of((1 - core) * half, 8), half)],
-            dst_ref=recv_a.at[b, pl.ds(0, half)],
-            send_sem=a_send.at[b], recv_sem=a_recv.at[b],
+            src_ref=g.at[b, at_core(b, p, 1 - core)],
+            dst_ref=recv_a.at[b, pl.ds(p * piece(b), piece(b))],
+            send_sem=a_send.at[b, p], recv_sem=a_recv.at[b, p],
             device_id=(me, other(1)), device_id_type=MESH,
         )
 
-    def stage_b(b, i):
-        half = rows_of(b) // 2
+    def stage_b(b, i, p):
+        rows = pl.ds(p * piece(b), piece(b))
         return pltpu.make_async_remote_copy(
-            src_ref=part.at[b, i, pl.ds(0, half)], dst_ref=recv_b.at[b, i, pl.ds(0, half)],
-            send_sem=b_send.at[b, i], recv_sem=b_recv.at[b, i],
+            src_ref=part.at[b, i, rows], dst_ref=recv_b.at[b, i, rows],
+            send_sem=b_send.at[b, i, p], recv_sem=b_recv.at[b, i, p],
             device_id=(me, other(1 << bits[i])), device_id_type=MESH,
         )
 
-    def stage_c(b):
-        half = rows_of(b) // 2
-        rows = pl.ds(pl.multiple_of(core * half, 8), half)
+    def stage_c(b, p):
+        rows = at_core(b, p, core)
         return pltpu.make_async_remote_copy(
             src_ref=fin.at[b, rows], dst_ref=fin.at[b, rows],
-            send_sem=c_send.at[b], recv_sem=c_recv.at[b],
+            send_sem=c_send.at[b, p], recv_sem=c_recv.at[b, p],
             device_id=(me, other(1)), device_id_type=MESH,
         )
 
+    def send_on(b, i, p, value):
+        if i < len(bits):
+            part[b, i, p * piece(b):(p + 1) * piece(b), :] = value
+            stage_b(b, i, p).start()
+        else:
+            fin[b, at_core(b, p, core), :] = value
+            stage_c(b, p).start()
+
     def after_a(b):
-        half = rows_of(b) // 2
-        stage_a(b).wait()
-        value = g[b, pl.ds(pl.multiple_of(core * half, 8), half), :] + recv_a[b, 0:half, :]
-        if bits:
-            part[b, 0, 0:half, :] = value
-            stage_b(b, 0).start()
-        else:
-            fin[b, pl.ds(pl.multiple_of(core * half, 8), half), :] = value
-            stage_c(b).start()
+        for p in range(PIECES):
+            stage_a(b, p).wait()
+            send_on(b, 0, p, g[b, at_core(b, p, core), :] + recv_a[b, p * piece(b):(p + 1) * piece(b), :])
 
     def after_b(b, i):
-        half = rows_of(b) // 2
-        stage_b(b, i).wait()
-        value = part[b, i, 0:half, :] + recv_b[b, i, 0:half, :]
-        if i + 1 < len(bits):
-            part[b, i + 1, 0:half, :] = value
-            stage_b(b, i + 1).start()
-        else:
-            fin[b, pl.ds(pl.multiple_of(core * half, 8), half), :] = value
-            stage_c(b).start()
+        for p in range(PIECES):
+            rows = slice(p * piece(b), (p + 1) * piece(b))
+            stage_b(b, i, p).wait()
+            send_on(b, i + 1, p, part[b, i, rows, :] + recv_b[b, i, rows, :])
 
     steps = []
     for b in range(layers):
@@ -326,7 +331,10 @@
         bias_row = first[2 * hid:2 * hid + 16] + second[hid:hid + 16]
         g[b, 0:hid, :] = first[0:hid] + first[hid:2 * hid] + second[0:hid]
         g[layers - 1, small + 4 + l:small + 5 + l, :] = bias_row[0:1]
-        stage_a(b).start()
+        for p in range(PIECES):
+            stage_a(b, p).start()
+        if b == 0:
+            head_grads()
         for earlier in range(b):
             if steps[earlier]:
                 steps[earlier].pop(0)()
@@ -346,7 +354,8 @@
             if steps[b]:
                 steps[b].pop(0)()
     for b in range(layers):
-        stage_c(b).wait()
+        for p in range(PIECES):
+            stage_c(b, p).wait()
 
 
 def unpack(pix_in, fin, pix_ref, gin_ref, gmid_ref, gout_ref, ghid_ref, gbout_ref, sems):
@@ -380,7 +389,7 @@
         delta = 3.0 / (SAMP * slabs)
         factor = 1.0 / math.sqrt(3.0 * n_rays * slabs * own)
         more = max(1, sum(1 for b in range(1, 16) if (1 << b) < n_rays))
-        half = (hid + 16) // 2
+        half = (hid + 32) // 2
         shape = jax.ShapeDtypeStruct
         args = (
             geometry, entry, counts, targets, w_in, w_mid, w_out,
@@ -389,7 +398,7 @@
         vmem = pl.BlockSpec(memory_space=pltpu.VMEM)
         pixels, packed = pl.pallas_call(
             functools.partial(kernel, slabs, n_rays, delta, factor),
-            out_shape=(pltpu.VMEM((3, own), F32), pltpu.VMEM((layers, hid + 16, hid), F32)),
+            out_shape=(pltpu.VMEM((3, own), F32), pltpu.VMEM((layers, hid + 32, hid), F32)),
             in_specs=[pl.BlockSpec(memory_space=pltpu.HBM)] * 10,
             out_specs=(vmem, vmem),
             scratch_shapes=[pltpu.VMEM(a.shape, a.dtype) for a in args] + [
@@ -400,19 +409,19 @@
                 pltpu.VMEM((layers, 2 * hid, hid), BF16),
                 pltpu.VMEM((mid, 2 * hid, hid), BF16),
                 pltpu.VMEM((slabs, 8, width), F32),
-                pltpu.VMEM((layers, hid + 16, hid), F32),
+                pltpu.VMEM((layers, hid + 32, hid), F32),
                 pltpu.VMEM((layers, half, hid), F32),
                 pltpu.VMEM((layers, more, half, hid), F32),
                 pltpu.VMEM((layers, more, half, hid), F32),
                 pltpu.SemaphoreType.DMA((10,)),
                 pltpu.SemaphoreType.DMA((slabs,)),
                 pltpu.SemaphoreType.DMA((slabs,)),
-                pltpu.SemaphoreType.DMA((layers,)),
-                pltpu.SemaphoreType.DMA((layers,)),
-                pltpu.SemaphoreType.DMA((layers, more)),
-                pltpu.SemaphoreType.DMA((layers, more)),
-                pltpu.SemaphoreType.DMA((layers,)),
-                pltpu.SemaphoreType.DMA((layers,)),
+                pltpu.SemaphoreType.DMA((layers, PIECES)),
+                pltpu.SemaphoreType.DMA((layers, PIECES)),
+                pltpu.SemaphoreType.DMA((layers, more, PIECES)),
+                pltpu.SemaphoreType.DMA((layers, more, PIECES)),
+                pltpu.SemaphoreType.DMA((layers, PIECES)),
+                pltpu.SemaphoreType.DMA((layers, PIECES)),
             ],
             compiler_params=pltpu.CompilerParams(
                 collective_id=0, has_side_effects=True, vmem_limit_bytes=58 * 1000 * 1024

time: 33.8 us -> 32.8 us (0.970)
  Pallas kernels: 33 us -> 31.9 us
    pallas_call x1, Pallas kernels: 31.5 us -> 30.4 us  [shards(): pl.pallas_call(functools.partial(kernel, slabs, n_rays, delta, factor), o...]
where the time goes in v4:
time: 32.8 us; the launch traced here: 32.6 us
  Pallas kernels  31.9 us (97%)
  between operations  0.64 us (2%)
    pallas_call x1, Pallas kernels, shards(): pl.pallas_call(functools.partial(kernel, slabs, n_rays, delta, factor), o...  30.4 us
    pallas_call x1, Pallas kernels, shards(): pl.pallas_call(unpack, out_shape=(shape((3, 1, own), F32), shape((1, 2 *...  1.5 us

profile of v4, /device:TPU:0, one launch (start us, length us, event | category | flops | bytes accessed | tf_op | source)
XLA Modules:
  0.0 32.6 jit_solution(7863615954399272820)
XLA Ops:
  0.6 30.4 %shard_map.145 = (f32[3,16]{1,0:T(4,128)S(1)}, f32[3,288,256]{2,1,0:T(8,128)S(1)}) custom-call(f32[6,1,128]{2,1,0:T(1,128)} %refs_0_.1, s32[1,1,128]{2,1,0:T(1,128)} %refs_1_.1, s32[1,1,128]{2,1,0:T(1,128)} %refs_2_.1, f32[3,1,16]{2,1,0:T(1,128)} %refs_3_.1, f32[1,256,256]{2,1,0:T(8,128)} %refs_4_.1, f32[1,2,256,256]{3,2,1,0:T(8,128)} %refs_5_.1, ...), custom_call_target="tpu_custom_call" | custom-call | tf_op jit(solution)/shard_map/pallas_call | solution.py:399
  31.1 1.5 %shard_map.146 = (f32[3,1,16]{2,1,0:T(1,128)}, f32[1,256,256]{2,1,0:T(8,128)}, f32[1,2,256,256]{3,2,1,0:T(8,128)}, f32[1,4,256]{2,1,0:T(4,128)}, f32[3,1,256]{2,1,0:T(1,128)}, /*index=5*/f32[1,4]{1,0:T(1,128)}) custom-call(f32[3,16]{1,0:T(4,128)S(1)} %get-tuple-element.14.pix_in, f32[3,288,256]{2,1,0:T(8,128)S(1)} %get-tuple-element.15.fin), custom_call_target="tpu_custom_call" | custom-call | tf_op jit(solution)/shard_map/pallas_call | solution.py:431

commit v5 on v4

--- a/solution.py
+++ b/solution.py
@@ -318,10 +318,6 @@
             stage_b(b, i, p).wait()
             send_on(b, i + 1, p, part[b, i, rows, :] + recv_b[b, i, rows, :])
 
-    steps = []
-    for b in range(layers):
-        steps.append([functools.partial(after_a, b)] + [functools.partial(after_b, b, i) for i in range(len(bits))])
-
     for b in range(layers):
         l = layers - 1 - b
         slot = b % 2
@@ -335,9 +331,6 @@
             stage_a(b, p).start()
         if b == 0:
             head_grads()
-        for earlier in range(b):
-            if steps[earlier]:
-                steps[earlier].pop(0)()
         if l > 0:
             def back(at, l=l, slot=slot):
                 lanes = pl.ds(at, chunk)
@@ -347,12 +340,10 @@
                 dh[1 - slot, :, lanes] = hi
                 dl[1 - slot, :, lanes] = lo
             chunks(back)
-            if steps[b]:
-                steps[b].pop(0)()
-    while any(steps):
+        after_a(b)
+    for i in range(len(bits)):
         for b in range(layers):
-            if steps[b]:
-                steps[b].pop(0)()
+            after_b(b, i)
     for b in range(layers):
         for p in range(PIECES):
             stage_c(b, p).wait()

time: 32.8 us -> 29.6 us (0.902)
  Pallas kernels: 31.9 us -> 28.8 us
    pallas_call x1, Pallas kernels: 30.4 us -> 27.3 us  [shards(): pl.pallas_call(functools.partial(kernel, slabs, n_rays, delta, factor), o...]
where the time goes in v5:
time: 29.6 us; the launch traced here: 29.4 us
  Pallas kernels  28.8 us (97%)
  between operations  0.64 us (2%)
    pallas_call x1, Pallas kernels, shards(): pl.pallas_call(functools.partial(kernel, slabs, n_rays, delta, factor), o...  27.3 us
    pallas_call x1, Pallas kernels, shards(): pl.pallas_call(unpack, out_shape=(shape((3, 1, own), F32), shape((1, 2 *...  1.5 us

profile of v5, /device:TPU:0, one launch (start us, length us, event | category | flops | bytes accessed | tf_op | source)
XLA Modules:
  0.0 29.4 jit_solution(10301127867757866951)
XLA Ops:
  0.6 27.3 %shard_map.145 = (f32[3,16]{1,0:T(4,128)S(1)}, f32[3,288,256]{2,1,0:T(8,128)S(1)}) custom-call(f32[6,1,128]{2,1,0:T(1,128)} %refs_0_.1, s32[1,1,128]{2,1,0:T(1,128)} %refs_1_.1, s32[1,1,128]{2,1,0:T(1,128)} %refs_2_.1, f32[3,1,16]{2,1,0:T(1,128)} %refs_3_.1, f32[1,256,256]{2,1,0:T(8,128)} %refs_4_.1, f32[1,2,256,256]{3,2,1,0:T(8,128)} %refs_5_.1, ...), custom_call_target="tpu_custom_call" | custom-call | tf_op jit(solution)/shard_map/pallas_call | solution.py:390
  28.0 1.5 %shard_map.146 = (f32[3,1,16]{2,1,0:T(1,128)}, f32[1,256,256]{2,1,0:T(8,128)}, f32[1,2,256,256]{3,2,1,0:T(8,128)}, f32[1,4,256]{2,1,0:T(4,128)}, f32[3,1,256]{2,1,0:T(1,128)}, /*index=5*/f32[1,4]{1,0:T(1,128)}) custom-call(f32[3,16]{1,0:T(4,128)S(1)} %get-tuple-element.14.pix_in, f32[3,288,256]{2,1,0:T(8,128)S(1)} %get-tuple-element.15.fin), custom_call_target="tpu_custom_call" | custom-call | tf_op jit(solution)/shard_map/pallas_call | solution.py:422
